TPU v7x, 32 devices: a whole 2x2x4 slice. The times are simulated.
32 devices in a mesh: group: 2 (over x), depth: 2 (over core), col: 8 (over z, y).
Axes of the slice: x: 2, y: 2, z: 4, core: 2. Of those that a mesh axis runs over, the one named last changes fastest.
Arguments:
- alignment_activations: bfloat16 [256, 32, 256], P(('group', 'depth'), 'col'), parts along dimension 0, may hold values from -8 to 8
- alignment_mask: int32 [256, 32], P(('group', 'depth'), 'col'), parts along dimension 0, may hold values from 0 to 1, as said below
- pair_activation_input: bfloat16 [64, 32, 128], P(('group', 'col'), 'depth'), parts along dimension 0, may hold values from -6 to 6
- pair_update_mask: int32 [64, 32], P(('group', 'col'), 'depth'), parts along dimension 0, may hold values 0 or 1
- pair_output_gradient: bfloat16 [64, 32, 128], P(('group', 'col'), 'depth'), parts along dimension 0, may hold values from -6 to 6
- layer_scale_factor: float32 [256], replicated, may hold values from 0.25 to 1.75
- first_projector: bfloat16 [256, 32], replicated, may hold values from -0.375 to 0.375
- second_projector: bfloat16 [256, 32], replicated, may hold values from -0.375 to 0.375
- output_weight: bfloat16 [1024, 128], replicated, may hold values from -1.5 to 1.5
- pair_norm_gain: float32 [128], replicated, may hold values from 0.25 to 1.75
- hidden_weight: bfloat16 [128, 512], replicated, may hold values from -0.5 to 0.5
- back_weight: bfloat16 [512, 128], replicated, may hold values from -0.25 to 0.25
Outputs:
- features_derivative: bfloat16 [256, 32, 256], P(('group', 'depth'), 'col'), parts along dimension 0
- couple_features_derivative: bfloat16 [64, 32, 128], P(('group', 'col'), 'depth'), parts along dimension 0
- first_projector_derivative: float32 [512, 32], P('group'), parts along dimension 0
- second_projector_derivative: float32 [512, 32], P('group'), parts along dimension 0
- result_matrix_derivative: float32 [2048, 128], P('group'), parts along dimension 0
- middle_matrix_derivative: float32 [256, 512], P('group'), parts along dimension 0
- final_matrix_derivative: float32 [1024, 128], P('group'), parts along dimension 0
There are 2 independent parts, one for each index of `group`. A program takes and returns all parts, laid end to end along the dimension named above; an argument that names none is the same for every part. Nothing has to cross between parts.
Inputs may be any that keep to these rules, and one draw needn't show every extreme that they name: `alignment_mask`: sequence 0 is present at every residue.
All inputs are finite; a program needn't handle non-finite values. No bound on the sum of `pair_update_mask` on one device may be relied on, other than what follows from the above.
Results may differ from a plain program's by a relative error of at most 0.014.
Values may be sent and summed in bfloat16 or wider, within the bound.
A program may use at most 64 MiB of HBM per device.

v0:
```python
import jax
import jax.numpy as jnp
from jax import lax
from jax.sharding import PartitionSpec as P

epsilon = 1e-05
highest = lax.Precision.HIGHEST


def norm_pieces(entries_drawn):
    center = entries_drawn - jnp.mean(entries_drawn, axis=-1, keepdims=True)
    inv_std = lax.rsqrt(jnp.mean(center * center, axis=-1, keepdims=True) + epsilon)
    return (center * inv_std, inv_std)


def standardize_adjoint(grad_scaled, scaled, inv_std):
    mean_grad = jnp.mean(grad_scaled, axis=-1, keepdims=True)
    mean_cross = jnp.mean(grad_scaled * scaled, axis=-1, keepdims=True)
    return inv_std * (grad_scaled - mean_grad - scaled * mean_cross)


def silu_pieces(pre_act):
    sigma = jax.nn.sigmoid(pre_act)
    return (pre_act * sigma, sigma * (1.0 + pre_act * (1.0 - sigma)))


def on_device(
    alignment_activations,
    alignment_mask,
    pair_activation_input,
    pair_update_mask,
    pair_output_gradient,
    layer_scale_factor,
    first_projector,
    second_projector,
    output_weight,
    pair_norm_gain,
    hidden_weight,
    back_weight,
):
    sequence_row_block, residue_row_block, channel_total = alignment_activations.shape
    proj_width = first_projector.shape[1]
    outer_width = proj_width * proj_width
    depth_count = lax.axis_size("depth")
    residues = residue_row_block * lax.axis_size("col")
    pair_cols = pair_activation_input.shape[1]
    pair_width = pair_activation_input.shape[2]
    col_block = min(64, pair_cols)
    block_count = pair_cols // col_block
    standardized_features, reciprocal_spread = norm_pieces(
        alignment_activations.astype(jnp.float32)
    )
    normalized_rows = (standardized_features * layer_scale_factor).astype(jnp.bfloat16)
    mask_floating = alignment_mask.astype(jnp.float32)
    left_proj = (
        jnp.dot(normalized_rows, first_projector, preferred_element_type=jnp.float32)
        * mask_floating[:, :, None]
    ).astype(jnp.bfloat16)
    right_proj = (
        jnp.dot(normalized_rows, second_projector, preferred_element_type=jnp.float32)
        * mask_floating[:, :, None]
    ).astype(jnp.bfloat16)
    right_flat = right_proj.reshape(sequence_row_block, residue_row_block * proj_width)
    mask_converted = alignment_mask.astype(jnp.bfloat16)
    seq_total = left_proj.shape[0]
    gathered, gathered_mask = (
        lax.all_gather(right_flat, "col", axis=1, tiled=True),
        lax.all_gather(mask_converted, "col", axis=1, tiled=True),
    )
    right_blocks = gathered.reshape(seq_total, depth_count, pair_cols, proj_width)
    mask_blocks = gathered_mask.reshape(seq_total, depth_count, pair_cols)
    block_depth = right_blocks.shape[1]
    out_wide = output_weight.astype(jnp.float32)

    def partial_outer(col_start):
        right_piece = lax.dynamic_slice_in_dim(right_blocks, col_start, col_block, 2)
        outer_part = jnp.einsum(
            "sic,sejd->iejcd", left_proj, right_piece, preferred_element_type=jnp.float32
        )
        return (
            outer_part.reshape(residue_row_block, block_depth, col_block, outer_width),
            right_piece,
        )

    def forward_step(step_index, loop_state):
        projected, pair_count = loop_state
        col_start = step_index * col_block
        outer_part, right_piece = partial_outer(col_start)
        mask_piece = lax.dynamic_slice_in_dim(mask_blocks, col_start, col_block, 2).astype(
            jnp.float32
        )
        count_part = jnp.einsum("si,sej->iej", mask_floating, mask_piece, precision=highest)
        outer_mine, count_mine = (
            lax.psum_scatter(
                outer_part.astype(jnp.bfloat16), "depth", scatter_dimension=1, tiled=True
            ).astype(jnp.float32),
            lax.psum_scatter(
                count_part.astype(jnp.bfloat16), "depth", scatter_dimension=1, tiled=True
            ).astype(jnp.float32),
        )
        proj_mine = jnp.dot(
            outer_mine.reshape(residue_row_block * col_block, outer_width),
            out_wide,
            precision=highest,
        )
        proj_mine = proj_mine.reshape(residue_row_block, col_block, pair_width)
        count_mine = count_mine.reshape(residue_row_block, col_block)
        projected = lax.dynamic_update_slice_in_dim(projected, proj_mine, col_start, 1)
        pair_count = lax.dynamic_update_slice_in_dim(pair_count, count_mine, col_start, 1)
        return (projected, pair_count)

    projected, pair_count = lax.fori_loop(
        0,
        block_count,
        forward_step,
        (
            jnp.zeros((residue_row_block, pair_cols, pair_width), jnp.float32),
            jnp.zeros((residue_row_block, pair_cols), jnp.float32),
        ),
    )
    count_column = pair_count.reshape(residue_row_block * pair_cols, 1)
    mid_act = (
        pair_activation_input.reshape(residue_row_block * pair_cols, pair_width).astype(jnp.float32)
        + projected.reshape(residue_row_block * pair_cols, pair_width) / count_column
    )
    pair_scaled, pair_inv = norm_pieces(mid_act)
    pair_normed = (pair_scaled * pair_norm_gain).astype(jnp.bfloat16)
    pre_act = jnp.dot(pair_normed, hidden_weight, preferred_element_type=jnp.float32)
    act_value, act_slope = silu_pieces(pre_act)
    hidden = act_value.astype(jnp.bfloat16)
    masked_grad = (
        pair_output_gradient * pair_update_mask.astype(jnp.bfloat16)[:, :, None]
    ).reshape(residue_row_block * pair_cols, pair_width)
    final_matrix_derivative = jnp.dot(hidden.T, masked_grad, preferred_element_type=jnp.float32)
    back_prod = jnp.dot(masked_grad, back_weight.T, preferred_element_type=jnp.float32)
    grad_hidden = (back_prod * act_slope).astype(jnp.bfloat16)
    middle_matrix_derivative = jnp.dot(
        pair_normed.T, grad_hidden, preferred_element_type=jnp.float32
    )
    grad_scaled = (
        jnp.dot(grad_hidden, hidden_weight.T, preferred_element_type=jnp.float32) * pair_norm_gain
    )
    grad_mid = pair_output_gradient.reshape(residue_row_block * pair_cols, pair_width).astype(
        jnp.float32
    ) + standardize_adjoint(grad_scaled, pair_scaled, pair_inv)
    couple_features_derivative = grad_mid.astype(jnp.bfloat16).reshape(
        residue_row_block, pair_cols, pair_width
    )
    grad_opm = (
        (grad_mid / count_column)
        .astype(jnp.bfloat16)
        .reshape(residue_row_block, pair_cols, pair_width)
    )
    full_opm = lax.all_gather(grad_opm, "depth", axis=1, tiled=True).reshape(
        residue_row_block, depth_count, pair_cols, pair_width
    )

    def backward_step(step_index, loop_state):
        grad_left_acc, grad_out, right_term = loop_state
        col_start = step_index * col_block
        outer_part, right_piece = partial_outer(col_start)
        opm_piece = lax.dynamic_slice_in_dim(full_opm, col_start, col_block, 2).reshape(
            residue_row_block * block_depth * col_block, pair_width
        )
        grad_out = grad_out + jnp.dot(
            outer_part.reshape(residue_row_block * block_depth * col_block, outer_width).T,
            opm_piece.astype(jnp.float32),
            precision=highest,
        )
        grad_outer = jnp.dot(opm_piece, output_weight.T, preferred_element_type=jnp.float32).astype(
            jnp.bfloat16
        )
        grad_outer = grad_outer.reshape(
            residue_row_block, block_depth, col_block, proj_width, proj_width
        )
        grad_left_acc = grad_left_acc + jnp.einsum(
            "iejcd,sejd->sic", grad_outer, right_piece, preferred_element_type=jnp.float32
        )
        piece_term = jnp.einsum(
            "iejcd,sic->ejsd", grad_outer, left_proj, preferred_element_type=jnp.float32
        )
        piece_term = piece_term.reshape(block_depth, col_block, seq_total * proj_width)
        right_term = lax.dynamic_update_slice_in_dim(right_term, piece_term, col_start, 1)
        return (grad_left_acc, grad_out, right_term)

    grad_left_acc, result_matrix_derivative, right_term = lax.fori_loop(
        0,
        block_count,
        backward_step,
        (
            jnp.zeros((seq_total, residue_row_block, proj_width), jnp.float32),
            jnp.zeros((outer_width, pair_width), jnp.float32),
            jnp.zeros((block_depth, pair_cols, seq_total * proj_width), jnp.float32),
        ),
    )
    grad_right_sum = lax.psum_scatter(
        right_term.reshape(residues, seq_total * proj_width), "col", scatter_dimension=0, tiled=True
    )
    grad_right_acc = jnp.transpose(
        grad_right_sum.reshape(residue_row_block, seq_total, proj_width), (1, 0, 2)
    )
    grad_left = (grad_left_acc * mask_floating[:, :, None]).astype(jnp.bfloat16)
    grad_right = (grad_right_acc * mask_floating[:, :, None]).astype(jnp.bfloat16)
    normed_rows = normalized_rows.reshape(sequence_row_block * residue_row_block, channel_total)
    first_projector_derivative = jnp.dot(
        normed_rows.T,
        grad_left.reshape(sequence_row_block * residue_row_block, proj_width),
        preferred_element_type=jnp.float32,
    )
    second_projector_derivative = jnp.dot(
        normed_rows.T,
        grad_right.reshape(sequence_row_block * residue_row_block, proj_width),
        preferred_element_type=jnp.float32,
    )
    standardized_derivative = jnp.dot(
        grad_left, first_projector.T, preferred_element_type=jnp.float32
    ) + jnp.dot(grad_right, second_projector.T, preferred_element_type=jnp.float32)
    features_derivative = standardize_adjoint(
        standardized_derivative * layer_scale_factor, standardized_features, reciprocal_spread
    ).astype(jnp.bfloat16)
    weight_sums = lax.psum(
        (
            first_projector_derivative,
            second_projector_derivative,
            result_matrix_derivative,
            middle_matrix_derivative,
            final_matrix_derivative,
        ),
        ("depth", "col"),
    )
    return (
        features_derivative,
        couple_features_derivative,
        weight_sums[0],
        weight_sums[1],
        weight_sums[2],
        weight_sums[3],
        weight_sums[4],
    )


def solution(mesh):
    in_specs = (
        P(("group", "depth"), "col", None),
        P(("group", "depth"), "col"),
        P(("group", "col"), "depth", None),
        P(("group", "col"), "depth"),
        P(("group", "col"), "depth", None),
        P(),
        P(),
        P(),
        P(),
        P(),
        P(),
        P(),
    )
    out_specs = (
        P(("group", "depth"), "col", None),
        P(("group", "col"), "depth", None),
        P("group", None),
        P("group", None),
        P("group", None),
        P("group", None),
        P("group", None),
    )
    return jax.shard_map(
        on_device, mesh=mesh, in_specs=in_specs, out_specs=out_specs, check_vma=False
    )
```

profile of v0, /device:TPU:0, one launch (start us, length us, event | category | flops | bytes accessed | tf_op | source)
XLA Modules:
  0.0 362.0 jit_solution(7298277247969911914)
XLA Ops:
  7.2 1.0 convert_reduce_fusion
  8.3 1.1 fusion.16
  10.2 1.2 fusion.4
  11.3 32.6 %all_gather.9 = bf16[64,1024]{0,1:T(8,128)(2,1)S(1)} all-gather(bf16[64,128]{0,1:T(8,128)(2,1)S(1)} %bitcast.138), channel_id=1, replica_groups=mesh['group'=2,'depth'=2,'col'=8] {'col'}, dimensions={1}, use_global_device_ids=true | all-gather | bytes 147456 | tf_op jit(solution)/shard_map/all_gather | solution.py:67
  43.9 1.2 fusion.5
  45.1 1.8 fusion.45
  47.5 1.9 convert_element_type.96
  49.5 20.6 %all-gather = bf16[8,4,64]{2,1,0:T(4,128)(2,1)S(1)} all-gather(bf16[1,4,64]{2,1,0:T(4,128)(2,1)S(1)} %get-tuple-element.95), channel_id=1, replica_groups=mesh['group'=2,'depth'=2,'col'=8] {'col'}, dimensions={0}, use_global_device_ids=true | all-gather | bytes 4608 | tf_op jit(solution)/shard_map/all_gather | solution.py:68
  70.2 2.5 all-reduce.1
  74.6 1.9 copy.35
  76.6 1.0 reshape.170
  78.3 1.6 constant_dynamic-slice_fusion.1
  82.3 0.9 fusion.17
  84.0 1.8 all_gather.11
  88.1 1.2 reshape.167
  90.3 1.4 fusion.47
  91.7 66.1 %all-reduce.12.cloned.1.call-done = f32[32,2048]{1,0:T(8,128)} async-done(((f32[32,2048]{1,0:T(8,128)}), f32[32,2048]{1,0:T(8,128)}) %all-reduce.12.cloned.1.call-update) | async-done | bytes 262160
  161.7 85.9 %all-reduce.14.cloned.1.call-done = (f32[256,32]{0,1:T(8,128)}, f32[256,32]{0,1:T(8,128)}) async-done(((f32[256,32]{0,1:T(8,128)}, f32[256,32]{0,1:T(8,128)}), (f32[256,32]{0,1:T(8,128)}, f32[256,32]{0,1:T(8,128)})) %all-reduce.14.cloned.1.call-update) | async-done | bytes 65552 | tf_op jit(solution)/shard_map/psum | solution.py:221
  247.6 99.9 %all-reduce.16.cloned.1.call-done = (f32[1024,128]{1,0:T(8,128)}, f32[128,512]{1,0:T(8,128)}, f32[512,128]{1,0:T(8,128)}) async-done(((f32[1024,128]{1,0:T(8,128)}, f32[128,512]{1,0:T(8,128)}, f32[512,128]{1,0:T(8,128)}), (f32[1024,128]{1,0:T(8,128)}, f32[128,512]{1,0:T(8,128)}, f32[512,128]{1,0:T(8,128)})) %all-reduce.16.cloned.1.call-update) | async-done | bytes 1048592 | tf_op jit(solution)/shard_map/psum | solution.py:221
  347.5 1.4 copy.62
  348.9 1.4 copy.63
  350.3 1.9 copy.64
  352.1 1.7 copy.65
  353.8 1.7 copy.66
  (79 shorter events, 13.7 us)
Async XLA Ops:
  7.2 72.7 %copy-start = (bf16[1024,128]{1,0:T(8,128)(2,1)S(1)}, bf16[1024,128]{1,0:T(8,128)(2,1)}, u32[]{:S(2)}) copy-start(bf16[1024,128]{1,0:T(8,128)(2,1)} %param.20) | copy-start | bytes 786436
  7.2 71.1 %all-reduce.10.cloned.1.call-start = ((), (), s32[]{:S(2)}) async-start(), calls=%async_computation | async-start | bytes 524288
  46.9 23.2 %copy-start.7 = (s32[64,4]{0,1:T(4,128)S(1)}, s32[64,4]{0,1:T(4,128)}, u32[]{:S(2)}) copy-start(s32[64,4]{0,1:T(4,128)} %param.13) | copy-start | bytes 3076
  46.9 25.8 %copy-start.13 = (u32[32]{0:T(128)S(1)}, u32[32]{0:T(128)}, u32[]{:S(2)}) copy-start(u32[32]{0:T(128)} %constant.47) | copy-start | bytes 388
  46.9 27.2 %copy-start.9 = (s32[4,16]{1,0:T(4,128)S(1)}, s32[4,16]{1,0:T(4,128)}, u32[]{:S(2)}) copy-start(s32[4,16]{1,0:T(4,128)} %param.15) | copy-start | bytes 772
  46.9 27.2 %copy-start.12 = (u32[32]{0:T(128)S(1)}, u32[32]{0:T(128)}, u32[]{:S(2)}) copy-start(u32[32]{0:T(128)} %constant.55) | copy-start | bytes 388
  49.4 108.4 %all-reduce.12.cloned.1.call-start = ((), (), s32[]{:S(2)}) async-start(), calls=%async_computation.1 | async-start | bytes 524288
  76.6 1.7 copy-start.4
  76.6 3.5 copy-start.3
  76.6 4.2 %copy-start.2 = (bf16[128,512]{1,0:T(8,128)(2,1)S(1)}, bf16[128,512]{1,0:T(8,128)(2,1)}, u32[]{:S(2)}) copy-start(bf16[128,512]{1,0:T(8,128)(2,1)} %param.22) | copy-start | bytes 393220
  76.6 4.1 %copy-start.8 = (f32[128]{0:T(128)S(1)}, f32[128]{0:T(128)}, u32[]{:S(2)}) copy-start(f32[128]{0:T(128)} %param.21) | copy-start | bytes 1540
  76.6 4.3 %copy-start.11 = (bf16[512,128]{1,0:T(8,128)(2,1)S(1)}, bf16[512,128]{1,0:T(8,128)(2,1)}, u32[]{:S(2)}) copy-start(bf16[512,128]{1,0:T(8,128)(2,1)} %param.23) | copy-start | bytes 393220
  87.3 2.1 copy-start.1
  87.3 2.1 copy-start.10
  88.1 71.7 %copy-start.5 = (bf16[256,32]{0,1:T(8,128)(2,1)S(1)}, bf16[256,32]{0,1:T(8,128)(2,1)}, u32[]{:S(2)}) copy-start(bf16[256,32]{0,1:T(8,128)(2,1)} %param.18) | copy-start | bytes 49156
  89.3 71.0 %copy-start.6 = (bf16[256,32]{0,1:T(8,128)(2,1)S(1)}, bf16[256,32]{0,1:T(8,128)(2,1)}, u32[]{:S(2)}) copy-start(bf16[256,32]{0,1:T(8,128)(2,1)} %param.19) | copy-start | bytes 49156
  89.3 158.3 %all-reduce.14.cloned.1.call-start = ((), (), s32[]{:S(2)}) async-start(), calls=%async_computation.2 | async-start | bytes 131072 | tf_op jit(solution)/shard_map/psum | solution.py:221
  159.7 187.8 %all-reduce.16.cloned.1.call-start = ((), (), s32[]{:S(2)}) async-start(), calls=%async_computation.3 | async-start | bytes 2097152 | tf_op jit(solution)/shard_map/psum | solution.py:221
Sparse Core Ops, SparseCore 0:
  49.5 19.2 all-reduce.9
  89.5 68.2 all-reduce.11
  161.9 85.6 all-reduce.13
  251.8 95.6 all-reduce.15
where the time goes:
time: 363 us; the launch traced here: 362 us
  waiting for transfers between devices  252 us (69%)
  blocking collectives  57.5 us (16%)
  local copies, waits for them, and re-layouts  20.5 us (6%)
  between operations  14.8 us (4%)
  matrix products  11.6 us (3%)
  other arithmetic  5.09 us (1%)
    psum x2, waiting for transfers between devices, on_device(): lax.psum((first_projector_derivative, second_projector_derivative, result...  186 us
    unnamed x6, waiting for transfers between devices  66.5 us
    all_gather x1, blocking collectives, on_device(): lax.all_gather(right_flat, 'col', axis=1, tiled=True)  32.6 us
    all_gather x1, blocking collectives, on_device(): lax.all_gather(mask_converted, 'col', axis=1, tiled=True)  20.6 us
    unnamed x38, local copies, waits for them, and re-layouts  12.4 us
  transfers between devices with their start and end apart: 4, of which 3 were waited for; matrix products, arithmetic and copies ran while one was open for 2% of the time, Pallas kernels for 0%

commit v1 on v0

--- a/solution.py
+++ b/solution.py
@@ -219,14 +219,17 @@
         standardized_derivative * layer_scale_factor, standardized_features, reciprocal_spread
     ).astype(jnp.bfloat16)
     weight_sums = lax.psum(
-        (
-            first_projector_derivative,
-            second_projector_derivative,
-            result_matrix_derivative,
-            middle_matrix_derivative,
-            final_matrix_derivative,
+        lax.psum(
+            (
+                first_projector_derivative,
+                second_projector_derivative,
+                result_matrix_derivative,
+                middle_matrix_derivative,
+                final_matrix_derivative,
+            ),
+            axis_name="col",
         ),
-        ("depth", "col"),
+        axis_name="depth",
     )
     return (
         features_derivative,

time: 363 us -> 301 us (0.83)
  waiting for transfers between devices: 252 us -> 191 us
    psum x2 -> x1, waiting for transfers between devices: 186 us -> 70.7 us  [on_device(): lax.psum((first_projector_derivative, second_projector_derivative, result...]
    psum x0 -> x2, waiting for transfers between devices: none -> 41 us  [on_device(): lax.psum(lax.psum((first_projector_derivative, second_projector_derivativ...]
    unnamed x6 -> x7, waiting for transfers between devices: 66.5 us -> 79.2 us
  transfers between devices with their start and end apart: 4 -> 5, of which waited for: 3 -> 4; matrix products, arithmetic and copies ran while one was open for 2% -> 3% of each run, Pallas kernels for 0% -> 0%
where the time goes in v1:
time: 301 us; the launch traced here: 300 us
  waiting for transfers between devices  191 us (63%)
  blocking collectives  57.5 us (19%)
  local copies, waits for them, and re-layouts  20.5 us (7%)
  between operations  14.8 us (5%)
  matrix products  11.6 us (4%)
  other arithmetic  5.09 us (2%)
    unnamed x7, waiting for transfers between devices  79.2 us
    psum x1, waiting for transfers between devices, on_device(): lax.psum((first_projector_derivative, second_projector_derivative, result...  70.7 us
    psum x2, waiting for transfers between devices, on_device(): lax.psum(lax.psum((first_projector_derivative, second_projector_derivativ...  41 us
    all_gather x1, blocking collectives, on_device(): lax.all_gather(right_flat, 'col', axis=1, tiled=True)  32.6 us
    all_gather x1, blocking collectives, on_device(): lax.all_gather(mask_converted, 'col', axis=1, tiled=True)  20.6 us
    unnamed x38, local copies, waits for them, and re-layouts  12.4 us
  transfers between devices with their start and end apart: 5, of which 4 were waited for; matrix products, arithmetic and copies ran while one was open for 3% of the time, Pallas kernels for 0%

profile of v1, /device:TPU:0, one launch (start us, length us, event | category | flops | bytes accessed | tf_op | source)
XLA Modules:
  0.0 300.5 jit_solution(3781440945031168000)
XLA Ops:
  7.2 1.0 convert_reduce_fusion
  8.3 1.1 fusion.16
  10.2 1.2 fusion.4
  11.3 32.6 %all_gather.9 = bf16[64,1024]{0,1:T(8,128)(2,1)S(1)} all-gather(bf16[64,128]{0,1:T(8,128)(2,1)S(1)} %bitcast.138), channel_id=1, replica_groups=mesh['group'=2,'depth'=2,'col'=8] {'col'}, dimensions={1}, use_global_device_ids=true | all-gather | bytes 147456 | tf_op jit(solution)/shard_map/all_gather | solution.py:67
  43.9 1.2 fusion.5
  45.1 1.8 fusion.45
  47.5 1.8 convert_element_type.96
  49.4 20.6 %all-gather = bf16[8,4,64]{2,1,0:T(4,128)(2,1)S(1)} all-gather(bf16[1,4,64]{2,1,0:T(4,128)(2,1)S(1)} %get-tuple-element.101), channel_id=1, replica_groups=mesh['group'=2,'depth'=2,'col'=8] {'col'}, dimensions={0}, use_global_device_ids=true | all-gather | bytes 4608 | tf_op jit(solution)/shard_map/all_gather | solution.py:68
  70.1 2.5 all-reduce.1
  73.9 1.9 copy.35
  75.9 1.0 reshape.170
  77.0 1.6 constant_dynamic-slice_fusion.1
  82.7 1.8 all_gather.11
  84.7 1.4 fusion.47
  87.7 1.2 reshape.167
  91.6 78.6 %all-reduce.17.cloned.1.call-done = (f32[32,2048]{1,0:T(8,128)}, f32[1024,128]{1,0:T(8,128)}, f32[128,512]{1,0:T(8,128)}, f32[512,128]{1,0:T(8,128)}) async-done(((f32[32,2048]{1,0:T(8,128)}, f32[1024,128]{1,0:T(8,128)}, f32[128,512]{1,0:T(8,128)}, f32[512,128]{1,0:T(8,128)}), (f32[32,2048]{1,0:T(8,128)}, f32[1024,128]{1,0:T(8,128)}, f32[128,512]{1,0:T(8,128)}, ...) | async-done | bytes 1310736
  172.2 70.7 %all-reduce.15.cloned.1.call-done = (f32[256,32]{0,1:T(8,128)}, f32[256,32]{0,1:T(8,128)}) async-done(((f32[256,32]{0,1:T(8,128)}, f32[256,32]{0,1:T(8,128)}), (f32[256,32]{0,1:T(8,128)}, f32[256,32]{0,1:T(8,128)})) %all-reduce.15.cloned.1.call-update) | async-done | bytes 65552 | tf_op jit(solution)/shard_map/psum | solution.py:222
  245.0 17.8 %all-reduce.19.cloned.1.call-done = (f32[256,32]{0,1:T(8,128)}, f32[256,32]{0,1:T(8,128)}) async-done(((f32[256,32]{0,1:T(8,128)}, f32[256,32]{0,1:T(8,128)}), (f32[256,32]{0,1:T(8,128)}, f32[256,32]{0,1:T(8,128)})) %all-reduce.19.cloned.1.call-update) | async-done | bytes 65552 | tf_op jit(solution)/shard_map/psum | solution.py:221
  262.8 23.2 %all-reduce.21.cloned.1.call-done = (f32[1024,128]{1,0:T(8,128)}, f32[128,512]{1,0:T(8,128)}, f32[512,128]{1,0:T(8,128)}) async-done(((f32[1024,128]{1,0:T(8,128)}, f32[128,512]{1,0:T(8,128)}, f32[512,128]{1,0:T(8,128)}), (f32[1024,128]{1,0:T(8,128)}, f32[128,512]{1,0:T(8,128)}, f32[512,128]{1,0:T(8,128)})) %all-reduce.21.cloned.1.call-update) | async-done | bytes 1048592 | tf_op jit(solution)/shard_map/psum | solution.py:221
  286.0 1.4 copy.67
  287.4 1.4 copy.68
  288.8 1.9 copy.69
  290.6 1.7 copy.70
  292.3 1.7 copy.71
  (82 shorter events, 14.9 us)
Async XLA Ops:
  7.2 71.4 %copy-start = (bf16[1024,128]{1,0:T(8,128)(2,1)S(1)}, bf16[1024,128]{1,0:T(8,128)(2,1)}, u32[]{:S(2)}) copy-start(bf16[1024,128]{1,0:T(8,128)(2,1)} %param.20) | copy-start | bytes 786436
  7.2 69.8 %all-reduce.13.cloned.1.call-start = ((), (), s32[]{:S(2)}) async-start(), calls=%async_computation | async-start | bytes 524288
  46.8 23.1 %copy-start.7 = (s32[64,4]{0,1:T(4,128)S(1)}, s32[64,4]{0,1:T(4,128)}, u32[]{:S(2)}) copy-start(s32[64,4]{0,1:T(4,128)} %param.13) | copy-start | bytes 3076
  46.8 25.8 %copy-start.13 = (u32[32]{0:T(128)S(1)}, u32[32]{0:T(128)}, u32[]{:S(2)}) copy-start(u32[32]{0:T(128)} %constant.47) | copy-start | bytes 388
  46.8 27.1 %copy-start.9 = (s32[4,16]{1,0:T(4,128)S(1)}, s32[4,16]{1,0:T(4,128)}, u32[]{:S(2)}) copy-start(s32[4,16]{1,0:T(4,128)} %param.15) | copy-start | bytes 772
  49.3 120.9 %all-reduce.17.cloned.1.call-start = ((), (), s32[]{:S(2)}) async-start(), calls=%async_computation.2 | async-start | bytes 2621440
  75.9 1.0 copy-start.4
  75.9 2.9 copy-start.3
  75.9 3.5 %copy-start.2 = (bf16[128,512]{1,0:T(8,128)(2,1)S(1)}, bf16[128,512]{1,0:T(8,128)(2,1)}, u32[]{:S(2)}) copy-start(bf16[128,512]{1,0:T(8,128)(2,1)} %param.22) | copy-start | bytes 393220
  75.9 3.5 %copy-start.8 = (f32[128]{0:T(128)S(1)}, f32[128]{0:T(128)}, u32[]{:S(2)}) copy-start(f32[128]{0:T(128)} %param.21) | copy-start | bytes 1540
  75.9 3.6 %copy-start.11 = (bf16[512,128]{1,0:T(8,128)(2,1)S(1)}, bf16[512,128]{1,0:T(8,128)(2,1)}, u32[]{:S(2)}) copy-start(bf16[512,128]{1,0:T(8,128)(2,1)} %param.23) | copy-start | bytes 393220
  87.3 1.7 copy-start.12
  87.7 3.0 copy-start.1
  87.7 3.0 copy-start.10
  89.0 154.5 %copy-start.5 = (bf16[256,32]{0,1:T(8,128)(2,1)S(1)}, bf16[256,32]{0,1:T(8,128)(2,1)}, u32[]{:S(2)}) copy-start(bf16[256,32]{0,1:T(8,128)(2,1)} %param.18) | copy-start | bytes 49156
  89.0 153.8 %all-reduce.15.cloned.1.call-start = ((), (), s32[]{:S(2)}) async-start(), calls=%async_computation.1 | async-start | bytes 131072 | tf_op jit(solution)/shard_map/psum | solution.py:222
  90.3 153.4 %copy-start.6 = (bf16[256,32]{0,1:T(8,128)(2,1)S(1)}, bf16[256,32]{0,1:T(8,128)(2,1)}, u32[]{:S(2)}) copy-start(bf16[256,32]{0,1:T(8,128)(2,1)} %param.19) | copy-start | bytes 49156
  172.1 90.7 %all-reduce.19.cloned.1.call-start = ((), (), s32[]{:S(2)}) async-start(), calls=%async_computation.3 | async-start | bytes 131072 | tf_op jit(solution)/shard_map/psum | solution.py:221
  242.8 43.2 %all-reduce.21.cloned.1.call-start = ((), (), s32[]{:S(2)}) async-start(), calls=%async_computation.4 | async-start | bytes 2097152 | tf_op jit(solution)/shard_map/psum | solution.py:221
Sparse Core Ops, SparseCore 0:
  49.4 19.2 all-reduce.12
  89.1 81.0 all-reduce.16
  174.3 68.5 all-reduce.14
  245.0 17.7 all-reduce.18
  265.1 20.8 all-reduce.20
